TPU v7x, 32 devices: a whole 2x2x4 slice. The times are simulated.
32 devices in a mesh: order: 8 (over z, x), chan: 4 (over y, core).
Axes of the slice: x: 2, y: 2, z: 4, core: 2. Of those that a mesh axis runs over, the one named last changes fastest.
Arguments:
- cotangent: bfloat16 [248, 240, 1, 2, 1024], P('order', None, None, None, 'chan'), may hold values from -0.59765625 to 0.59765625
- stored_coefficients: bfloat16 [248, 240, 1, 2, 1024], P('order', None, None, None, 'chan'), may hold values from -0.29882812 to 0.29882812
- weights: bfloat16 [248, 1024, 1024], P('order', 'chan'), may hold values from -0.1875 to 0.1875
- order_table: int32 [248], replicated, may hold values from 0 to 240, as said below
- degree_table: int32 [248], replicated, may hold values from 0 to 240, as said below
Outputs:
- input_gradient: bfloat16 [248, 240, 1, 2, 1024], P('order', None, None, None, 'chan')
- mixing_gradient: bfloat16 [248, 1024, 1024], P('order', 'chan')
Inputs may be any that keep to these rules, and one draw needn't show every extreme that they name: `order_table`: each order 0 to 239 stands in exactly one slot; every other slot holds 240, meaning empty. `degree_table`: each degree 0 to 239 stands in exactly one slot; every other slot holds 240, meaning empty.
All inputs are finite; a program needn't handle non-finite values.
Results may differ from a plain program's by a relative error of at most 0.008.
Values may be sent and summed in bfloat16 or wider, within the bound.
A program may use at most 192 MiB of HBM per device.

v0:
```python
import jax
import jax.numpy as jnp
from jax import lax
from jax.sharding import PartitionSpec as P


def legendre_rows(orders, degree_range, latitude_count):
    order_real = orders.astype(jnp.float32)[:, None]
    angles = jnp.pi * (jnp.arange(latitude_count).astype(jnp.float32) + 0.5) / latitude_count
    cosine = jnp.cos(angles)[None, :]
    sine = jnp.sin(angles)[None, :]
    counter = jnp.arange(1, degree_range + 1).astype(jnp.float32)
    factors = jnp.log((2.0 * counter - 1.0) / (2.0 * counter))
    below = (counter[None, :] <= order_real).astype(jnp.float32)
    log_start = 0.5 * (
        jnp.log((2.0 * order_real + 1.0) / (4.0 * jnp.pi))
        + jnp.sum(below * factors[None, :], axis=1, keepdims=True)
    )
    parity = 1.0 - 2.0 * (orders % 2).astype(jnp.float32)[:, None]
    start = parity * jnp.exp(log_start + order_real * jnp.log(sine))

    def advance(carry, degree):
        latest, before = carry
        level = degree.astype(jnp.float32)
        upper = jnp.sqrt(
            jnp.maximum(4.0 * level * level - 1.0, 0.0)
            / jnp.maximum(level * level - order_real * order_real, 1.0)
        )
        lower = jnp.sqrt(
            jnp.maximum((level - 1.0) * (level - 1.0) - order_real * order_real, 0.0)
            / jnp.maximum(4.0 * (level - 1.0) * (level - 1.0) - 1.0, 1.0)
        )
        grown = upper * (cosine * latest - lower * before)
        fresh = jnp.where(
            level == order_real, start, jnp.where(level > order_real, grown, jnp.zeros_like(grown))
        )
        return ((fresh, latest), fresh)

    zeros = jnp.zeros((orders.shape[0], latitude_count), jnp.float32)
    unused_result, stacked = lax.scan(advance, (zeros, zeros), jnp.arange(degree_range))
    return jnp.transpose(stacked, (1, 0, 2))


def quadrature(latitude_count):
    angles = jnp.pi * (jnp.arange(latitude_count).astype(jnp.float32) + 0.5) / latitude_count
    return jnp.pi / latitude_count * jnp.sin(angles)


def per_device(cotangent, stored_coefficients, weights, order_table, degree_table):
    slots, latitude_count, batch_size, unused_result, slot_width = cotangent.shape
    degree_range = stored_coefficients.shape[1]
    peers = lax.axis_size("order")
    position = lax.axis_index("order")
    mine = lax.dynamic_slice_in_dim(order_table, position * slots, slots)
    table = legendre_rows(mine, degree_range, latitude_count)
    table_halfprecision = table.astype(jnp.bfloat16)
    flat_cotangent = cotangent.reshape(slots, latitude_count, batch_size * 2 * slot_width)
    adjoint = jnp.einsum(
        "slj,sjf->slf", table_halfprecision, flat_cotangent, preferred_element_type=jnp.float32
    ).astype(jnp.bfloat16)
    adjoint = adjoint.reshape(slots, degree_range, batch_size * 2, slot_width)
    active_mask = jnp.arange(degree_range)[None, :] >= mine[:, None]
    masked_values = stored_coefficients.reshape(
        slots, degree_range, batch_size * 2, slot_width
    ) * active_mask[:, :, None, None].astype(jnp.bfloat16)
    clipped = jnp.minimum(degree_table, degree_range - 1)
    valid = (degree_table[None, :] >= mine[:, None]) & (degree_table[None, :] < degree_range)
    valid_bf = valid.astype(jnp.bfloat16)

    def pack_rows(source):
        picked = jnp.take(source, clipped, axis=1) * valid_bf[:, :, None, None]
        return picked.reshape(slots, peers, slots, batch_size * 2, source.shape[3])

    send_adjoint = pack_rows(adjoint)
    send_saved = pack_rows(masked_values)
    recv_saved, recv_adjoint = (
        lax.all_to_all(send_saved, "order", split_axis=1, concat_axis=1, tiled=True),
        lax.all_to_all(send_adjoint, "order", split_axis=1, concat_axis=1, tiled=True),
    )
    recv_adjoint = lax.all_gather(recv_adjoint, "chan", axis=4, tiled=True)
    mixing_gradient = jnp.einsum(
        "sntrc,sntrd->tcd", recv_saved, recv_adjoint, preferred_element_type=jnp.float32
    ).astype(jnp.bfloat16)
    coefficient_gradient = jnp.einsum(
        "sntrd,tcd->sntrc", recv_adjoint, weights, preferred_element_type=jnp.float32
    ).astype(jnp.bfloat16)
    returned = lax.all_to_all(
        coefficient_gradient, "order", split_axis=1, concat_axis=1, tiled=True
    )
    returned = returned.reshape(slots, peers * slots, batch_size * 2 * slot_width)
    picked_table = jnp.take(table_halfprecision, clipped, axis=1) * valid_bf[:, :, None]
    summed = jnp.einsum("skj,skf->sjf", picked_table, returned, preferred_element_type=jnp.float32)
    quad = quadrature(latitude_count)
    input_gradient = (summed * quad[None, :, None]).astype(jnp.bfloat16)
    return (
        input_gradient.reshape(slots, latitude_count, batch_size, 2, slot_width),
        mixing_gradient,
    )


def solution(mesh):
    return jax.shard_map(
        per_device,
        mesh=mesh,
        in_specs=(
            P("order", None, None, None, "chan"),
            P("order", None, None, None, "chan"),
            P("order", "chan", None),
            P(),
            P(),
        ),
        out_specs=(P("order", None, None, None, "chan"), P("order", "chan", None)),
        check_vma=False,
    )
```

profile of v0, /device:TPU:0, one launch (start us, length us, event | category | flops | bytes accessed | tf_op | source)
XLA Modules:
  0.0 1297.3 jit_solution(11286440266197965360)
XLA Ops:
  7.3 0.8 fusion.22
  9.7 491.0 %while.18 = (s32[]{:T(128)}, f32[31,240]{1,0:T(8,128)S(1)}, f32[31,240]{1,0:T(8,128)S(1)}, bf16[240,31,240]{2,1,0:T(8,128)(2,1)}, s32[240]{0:T(256)S(1)}, /*inde...) while((s32[]{:T(128)}, f32[31,240]{1,0:T(8,128)S(1)}, ...), condition=%wide.region_2.3_spmd.clone, body=%wide.region_1.2_spmd.clone.sunk | while | flops 75383 | bytes 156779 | solution.py:40
  15.2 0.7 bitcast_dynamic-update-slice_fusion.2
  31.5 0.7 bitcast_dynamic-update-slice_fusion.2
  95.0 0.7 bitcast_dynamic-update-slice_fusion.2
  176.8 0.7 bitcast_dynamic-update-slice_fusion.2
  244.3 0.7 bitcast_dynamic-update-slice_fusion.2
  283.2 0.7 bitcast_dynamic-update-slice_fusion.2
  381.4 0.7 bitcast_dynamic-update-slice_fusion.2
  440.7 0.7 bitcast_dynamic-update-slice_fusion.2
  500.8 17.3 %reshape.244 = bf16[31,240,512]{2,1,0:T(8,128)(2,1)} reshape(bf16[31,240,1,2,256]{4,3,2,1,0:T(2,128)(2,1)} %param.9) | data formatting | bytes 15237120 | tf_op jit(solution)/shard_map/reshape | solution.py:57
  518.1 12.3 convolution_convert_fusion
  530.4 16.2 %reshape.245 = bf16[31,240,2,256]{3,2,1,0:T(2,128)(2,1)} reshape(bf16[31,240,512]{2,1,0:T(8,128)(2,1)} %convolution_convert_fusion) | data formatting | bytes 15237120 | tf_op jit(solution)/shard_map/reshape | solution.py:61
  546.6 28.1 %gather_fusion.1 = bf16[248,31,2,256]{3,2,1,0:T(2,128)(2,1)} fusion(bf16[31,240,2,256]{3,2,1,0:T(2,128)(2,1)} %reshape.245, s32[1024]{0:T(1024)S(1)} %pad_clamp_fusion), kind=kCustom, calls=%fused_computation.clone | custom fusion | bytes 15746016 | tf_op jit(solution)/shard_map/jit(_take)/gather | solution.py:71
  574.7 11.6 bitcast_multiply_fusion.2
  586.3 39.2 %gather_fusion.2 = bf16[248,31,2,256]{3,2,1,0:T(2,128)(2,1)} fusion(bf16[31,240,2,256]{3,2,1,0:T(2,128)(2,1)} %bitcast_multiply_fusion.2, s32[1024]{0:T(1024)S(1)} %pad_clamp_fusion), kind=kCustom, calls=%fused_computation.1.clone | custom fusion | bytes 15746016 | tf_op jit(solution)/shard_map/jit(_take)/gather | solution.py:71
  625.6 20.7 %bitcast_multiply_fusion = (bf16[31,248,2,256]{3,2,0,1:T(2,128)(2,1)}, bf16[31,248,2,256]{3,2,0,1:T(2,128)(2,1)S(1)}) fusion(bf16[248,31,2,256]{3,2,1,0:T(2,128)(2,1)} %gather_fusion.2, pred[248]{0:T(512)(128)(4,1)S(1)} %get-tuple-element.223, bf16[31,248]{0,1:T(8,128)(2,1)S(1)} %and_convert_fusion, bf16[248,31,2,256]{3,2,1,0:T(2,128)(2,1)} %gather_fusion.1), kind=kLoop, calls=%fused_computation.22 | loop fusion | flops 15745024 | bytes 31505672 | tf_op jit(solution)/shard_map/mul | solution.py:71
  646.3 179.9 %all_to_all.15 = bf16[31,8,31,2,256]{4,3,0,2,1:T(2,128)(2,1)S(1)} all-to-all(bf16[31,8,31,2,256]{4,3,0,2,1:T(2,128)(2,1)S(1)} %bitcast.58), channel_id=1, replica_groups=mesh['order'=8,'chan'=4] {'order'}, dimensions={1} | all-to-all | bytes 15745024 | tf_op jit(solution)/shard_map/all_to_all | solution.py:78
  826.2 5.4 copy.23
  831.6 7.7 copy.28
  839.2 5.1 all-to-all-start.2
  844.4 6.8 gather_fusion
  851.7 6.0 bitcast_multiply_fusion.3
  857.8 166.1 %all-gather.2.cloned.1.call-done = bf16[31,8,31,2,1024]{4,1,3,0,2:T(8,128)(2,1)} async-done(((bf16[31,8,31,2,256]{4,1,3,0,2:T(8,128)(2,1)}), bf16[31,8,31,2,1024]{4,1,3,0,2:T(8,128)(2,1)}) %all-gather.2.cloned.1.call-update) | async-done | bytes 31490064 | tf_op jit(solution)/shard_map/all_gather | solution.py:80
  1023.9 19.6 %convert_bitcast_fusion = bf16[31,8,31,2,256]{4,1,3,0,2:T(8,128)(2,1)} fusion(bf16[31,8,31,2,1024]{4,1,3,0,2:T(8,128)(2,1)} %all-gather.2.cloned.1.call-done, bf16[31,256,1024]{2,1,0:T(8,128)(2,1)} %param.11), kind=kOutput, calls=%fused_computation.25 | convolution fusion | flops 8065388544 | bytes 55615488 | tf_op jit(solution)/shard_map/sntrd,tcd->sntrc/dot_general | solution.py:84
  1043.6 12.8 copy.24
  1056.4 5.5 all-to-all-start.1
  1061.9 23.4 %bitcast_convert_fusion = bf16[31,256,1024]{2,1,0:T(8,128)(2,1)} fusion(bf16[31,8,31,2,1024]{4,1,3,0,2:T(8,128)(2,1)} %all-gather.2.cloned.1.call-done, bf16[31,8,31,2,256]{4,3,2,0,1:T(2,128)(2,1)} %all-to-all-done.2), kind=kOutput, calls=%fused_computation.13 | convolution fusion | flops 8069578752 | bytes 55615488 | tf_op jit(solution)/shard_map/sntrc,sntrd->tcd/dot_general | solution.py:81
  1085.3 149.1 %all-to-all-done.1 = bf16[31,8,31,2,256]{4,3,0,2,1:T(2,128)(2,1)} async-done(((bf16[31,8,31,2,256]{4,3,0,2,1:T(2,128)(2,1)}), bf16[31,8,31,2,256]{4,3,0,2,1:T(2,128)(2,1)}, u32[]{:S(2)}, u32[]{:S(2)}) %all-to-all-start.1) | async-done | bytes 7872544 | tf_op jit(solution)/shard_map/all_to_all | solution.py:87
  1234.4 17.8 %reshape.284 = bf16[31,248,512]{2,0,1:T(8,128)(2,1)} reshape(bf16[31,8,31,2,256]{4,3,0,2,1:T(2,128)(2,1)} %all-to-all-done.1) | data formatting | bytes 15745024 | tf_op jit(solution)/shard_map/reshape | solution.py:90
  1252.2 21.6 %multiply_convert_fusion = bf16[31,240,512]{2,1,0:T(8,128)(2,1)} fusion(bf16[31,248,512]{2,0,1:T(8,128)(2,1)} %reshape.284, f32[240]{0:T(256)S(1)} %copy-done.1, bf16[31,248,240]{2,0,1:T(8,128)(2,1)} %bitcast_multiply_fusion.3), kind=kOutput, calls=%fused_computation.20 | convolution fusion | flops 1897021440 | bytes 19182272 | tf_op jit(solution)/shard_map/skj,skf->sjf/dot_general | solution.py:92
  1273.8 16.2 %reshape.248 = bf16[31,240,1,2,256]{4,3,1,0,2:T(2,128)(2,1)} reshape(bf16[31,240,512]{2,1,0:T(8,128)(2,1)} %multiply_convert_fusion) | data formatting | bytes 15237120 | tf_op jit(solution)/shard_map/reshape | solution.py:96
  (1215 shorter events, 323.7 us)
Async XLA Ops:
  7.2 1016.8 %all-gather.2.cloned.1.call-start = ((), (), s32[]{:S(2)}) async-start(), calls=%async_computation.3 | async-start | bytes 39362560 | tf_op jit(solution)/shard_map/all_gather | solution.py:80
  586.3 39.2 %copy-start = (s32[248]{0:T(256)S(1)}, s32[248]{0:T(256)}, u32[]{:S(2)}) copy-start(s32[248]{0:T(256)} %param.13) | copy-start | bytes 2980
  839.2 217.1 %all-to-all-start.2 = ((bf16[31,8,31,2,256]{4,3,2,0,1:T(2,128)(2,1)}), bf16[31,8,31,2,256]{4,3,2,0,1:T(2,128)(2,1)}, u32[]{:S(2)}, u32[]{:S(2)}) async-start(bf16[31,8,31,2,256]{4,3,2,0,1:T(2,128)(2,1)} %copy.28), calls=%async_computation.2 | async-start | bytes 15745024 | tf_op jit(solution)/shard_map/all_to_all | solution.py:77
  1056.4 178.0 %all-to-all-start.1 = ((bf16[31,8,31,2,256]{4,3,0,2,1:T(2,128)(2,1)}), bf16[31,8,31,2,256]{4,3,0,2,1:T(2,128)(2,1)}, u32[]{:S(2)}, u32[]{:S(2)}) async-start(bf16[31,8,31,2,256]{4,3,0,2,1:T(2,128)(2,1)} %copy.24), calls=%async_computation.1 | async-start | bytes 15745024 | tf_op jit(solution)/shard_map/all_to_all | solution.py:87
  1085.3 166.9 %copy-start.1 = (f32[240]{0:T(256)S(1)}, f32[240]{0:T(256)}, u32[]{:S(2)}) copy-start(f32[240]{0:T(256)} %fusion.18) | copy-start | bytes 2884
Sparse Core Ops, SparseCore 0:
  831.7 192.1 all-gather.1
where the time goes:
time: 1310 us; the launch traced here: 1300 us
  waiting for transfers between devices  315 us (24%)
  local copies, waits for them, and re-layouts  307 us (23%)
  other arithmetic  229 us (17%)
  blocking collectives  180 us (14%)
  loops' own time  164 us (13%)
  matrix products  76.9 us (6%)
  between operations  14.5 us (1%)
    all_to_all x1, blocking collectives, per_device(): lax.all_to_all(send_adjoint, 'order', split_axis=1, concat_axis=1, tiled=...  180 us
    dynamic_update_slice x240, other arithmetic, legendre_rows(): lax.scan(advance, (zeros, zeros), jnp.arange(degree_range))  169 us
    all_gather x1, waiting for transfers between devices, per_device(): recv_adjoint = lax.all_gather(recv_adjoint, 'chan', axis=4, tiled=True)  166 us
    another operation x1, loops' own time, legendre_rows(): lax.scan(advance, (zeros, zeros), jnp.arange(degree_range))  164 us
    all_to_all x1, waiting for transfers between devices, per_device(): lax.all_to_all(coefficient_gradient, 'order', split_axis=1, concat_axis=1...  149 us
    dynamic_slice x240, local copies, waits for them, and re-layouts, legendre_rows(): lax.scan(advance, (zeros, zeros), jnp.arange(degree_range))  140 us
    gather x2, local copies, waits for them, and re-layouts, pack_rows(): picked = jnp.take(source, clipped, axis=1) * valid_bf[:, :, None, None]  67.3 us
  transfers between devices with their start and end apart: 3, of which 2 were waited for; matrix products, arithmetic and copies ran while one was open for 6% of the time, Pallas kernels for 0%

commit v1 on v0

--- a/solution.py
+++ b/solution.py
@@ -84,8 +84,14 @@
     coefficient_gradient = jnp.einsum(
         "sntrd,tcd->sntrc", recv_adjoint, weights, preferred_element_type=jnp.float32
     ).astype(jnp.bfloat16)
-    returned = lax.all_to_all(
-        coefficient_gradient, "order", split_axis=1, concat_axis=1, tiled=True
+    returned = jnp.concatenate(
+        lax.all_to_all(
+            jnp.stack(jnp.split(coefficient_gradient, lax.axis_size("order"), axis=1)),
+            "order",
+            0,
+            0,
+        ),
+        axis=1,
     )
     returned = returned.reshape(slots, peers * slots, batch_size * 2 * slot_width)
     picked_table = jnp.take(table_halfprecision, clipped, axis=1) * valid_bf[:, :, None]

time: 1310 us -> 1340 us (1.023)
  local copies, waits for them, and re-layouts: 307 us -> 344 us
    split x0 -> x1, local copies, waits for them, and re-layouts: none -> 27.5 us  [per_device(): jnp.split(coefficient_gradient, lax.axis_size('order'), axis=1)]
    another operation x1 -> x4, local copies, waits for them, and re-layouts: 0.01 us -> 26.7 us  [the longest x1 17.9 us: per_device(): returned.reshape(slots, peers * slots, batch_size * 2 * slot_width)]
  transfers between devices with their start and end apart: 3 -> 3, of which waited for: 2 -> 2; matrix products, arithmetic and copies ran while one was open for 6% -> 8% of each run, Pallas kernels for 0% -> 0%
where the time goes in v1:
time: 1340 us; the launch traced here: 1330 us
  local copies, waits for them, and re-layouts  344 us (26%)
  waiting for transfers between devices  315 us (24%)
  other arithmetic  230 us (17%)
  blocking collectives  180 us (13%)
  loops' own time  163 us (12%)
  matrix products  69.2 us (5%)
  between operations  14.5 us (1%)
    all_to_all x1, blocking collectives, per_device(): lax.all_to_all(send_adjoint, 'order', split_axis=1, concat_axis=1, tiled=...  180 us
    dynamic_update_slice x240, other arithmetic, legendre_rows(): lax.scan(advance, (zeros, zeros), jnp.arange(degree_range))  169 us
    all_gather x1, waiting for transfers between devices, per_device(): recv_adjoint = lax.all_gather(recv_adjoint, 'chan', axis=4, tiled=True)  166 us
    another operation x1, loops' own time, legendre_rows(): lax.scan(advance, (zeros, zeros), jnp.arange(degree_range))  163 us
    all_to_all x1, waiting for transfers between devices, per_device(): lax.all_to_all(jnp.stack(jnp.split(coefficient_gradient, lax.axis_size('o...  149 us
    dynamic_slice x240, local copies, waits for them, and re-layouts, legendre_rows(): lax.scan(advance, (zeros, zeros), jnp.arange(degree_range))  140 us
    gather x2, local copies, waits for them, and re-layouts, pack_rows(): picked = jnp.take(source, clipped, axis=1) * valid_bf[:, :, None, None]  67.7 us
    split x1, local copies, waits for them, and re-layouts, per_device(): jnp.split(coefficient_gradient, lax.axis_size('order'), axis=1)  27.5 us
  transfers between devices with their start and end apart: 3, of which 2 were waited for; matrix products, arithmetic and copies ran while one was open for 8% of the time, Pallas kernels for 0%

profile of v1, /device:TPU:0, one launch (start us, length us, event | category | flops | bytes accessed | tf_op | source)
XLA Modules:
  0.0 1325.9 jit_solution(6259484131569808004)
XLA Ops:
  8.7 0.8 fusion.21
  9.7 0.8 and_convert_fusion
  10.5 490.0 %while.18 = (s32[]{:T(128)}, f32[31,240]{1,0:T(8,128)S(1)}, f32[31,240]{1,0:T(8,128)S(1)}, bf16[240,31,240]{2,1,0:T(8,128)(2,1)}, s32[240]{0:T(256)S(1)}, /*inde...) while((s32[]{:T(128)}, f32[31,240]{1,0:T(8,128)S(1)}, ...), condition=%wide.region_2.3_spmd.clone, body=%wide.region_1.2_spmd.clone.sunk | while | flops 75383 | bytes 156279 | solution.py:40
  103.8 0.7 bitcast_dynamic-update-slice_fusion.10
  138.5 0.7 bitcast_dynamic-update-slice_fusion.10
  361.0 0.7 bitcast_dynamic-update-slice_fusion.10
  500.6 17.3 %reshape.244 = bf16[31,240,512]{2,1,0:T(8,128)(2,1)} reshape(bf16[31,240,1,2,256]{4,3,2,1,0:T(2,128)(2,1)} %param.9) | data formatting | bytes 15237120 | tf_op jit(solution)/shard_map/reshape | solution.py:57
  517.9 12.3 convolution_convert_fusion
  530.1 16.2 %reshape.245 = bf16[31,240,2,256]{3,2,1,0:T(2,128)(2,1)} reshape(bf16[31,240,512]{2,1,0:T(8,128)(2,1)} %convolution_convert_fusion) | data formatting | bytes 15237120 | tf_op jit(solution)/shard_map/reshape | solution.py:61
  546.4 11.6 bitcast_multiply_fusion.2
  557.9 28.1 %gather_fusion.2 = bf16[248,31,2,256]{3,2,1,0:T(2,128)(2,1)} fusion(bf16[31,240,2,256]{3,2,1,0:T(2,128)(2,1)} %bitcast_multiply_fusion.2, s32[1024]{0:T(1024)S(1)} %pad_clamp_fusion), kind=kCustom, calls=%fused_computation.1.clone | custom fusion | bytes 15746016 | tf_op jit(solution)/shard_map/jit(_take)/gather | solution.py:71
  586.1 39.6 %gather_fusion.1 = bf16[248,31,2,256]{3,2,1,0:T(2,128)(2,1)} fusion(bf16[31,240,2,256]{3,2,1,0:T(2,128)(2,1)} %reshape.245, s32[1024]{0:T(1024)S(1)} %pad_clamp_fusion), kind=kCustom, calls=%fused_computation.clone | custom fusion | bytes 15746016 | tf_op jit(solution)/shard_map/jit(_take)/gather | solution.py:71
  625.7 20.6 %bitcast_multiply_fusion = (bf16[31,248,2,256]{3,2,0,1:T(2,128)(2,1)}, bf16[31,248,2,256]{3,2,0,1:T(2,128)(2,1)S(1)}) fusion(bf16[248,31,2,256]{3,2,1,0:T(2,128)(2,1)} %gather_fusion.2, pred[248]{0:T(512)(128)(4,1)S(1)} %get-tuple-element.245, bf16[31,248]{0,1:T(8,128)(2,1)S(1)} %and_convert_fusion, bf16[248,31,2,256]{3,2,1,0:T(2,128)(2,1)} %gather_fusion.1), kind=kLoop, calls=%fused_computation.22 | loop fusion | flops 15745024 | bytes 31505672 | tf_op jit(solution)/shard_map/mul | solution.py:71
  646.3 179.9 %all_to_all.15 = bf16[31,8,31,2,256]{4,3,0,2,1:T(2,128)(2,1)S(1)} all-to-all(bf16[31,8,31,2,256]{4,3,0,2,1:T(2,128)(2,1)S(1)} %bitcast.76), channel_id=1, replica_groups=mesh['order'=8,'chan'=4] {'order'}, dimensions={1} | all-to-all | bytes 15745024 | tf_op jit(solution)/shard_map/all_to_all | solution.py:78
  826.2 5.3 copy.172
  831.5 7.7 copy.185
  839.2 5.1 all-to-all-start.2
  844.3 6.8 gather_fusion
  851.8 6.0 bitcast_multiply_fusion.3
  857.8 166.1 %all-gather.2.cloned.1.call-done = bf16[31,8,31,2,1024]{4,1,3,0,2:T(8,128)(2,1)} async-done(((bf16[31,8,31,2,256]{4,1,3,0,2:T(8,128)(2,1)}), bf16[31,8,31,2,1024]{4,1,3,0,2:T(8,128)(2,1)}) %all-gather.2.cloned.1.call-update) | async-done | bytes 31490064 | tf_op jit(solution)/shard_map/all_gather | solution.py:80
  1023.9 19.6 %convert_bitcast_fusion = bf16[31,8,31,2,256]{4,1,3,0,2:T(8,128)(2,1)} fusion(bf16[31,8,31,2,1024]{4,1,3,0,2:T(8,128)(2,1)} %all-gather.2.cloned.1.call-done, bf16[31,256,1024]{2,1,0:T(8,128)(2,1)} %param.11), kind=kOutput, calls=%fused_computation.24 | convolution fusion | flops 8065388544 | bytes 55615488 | tf_op jit(solution)/shard_map/sntrd,tcd->sntrc/dot_general | solution.py:84
  1043.5 27.5 %fusion.23 = (bf16[31,1,31,2,256]{4,1,3,0,2:T(2,128)(2,1)S(1)}, bf16[31,1,31,2,256]{4,1,3,0,2:T(2,128)(2,1)S(1)}, bf16[31,1,31,2,256]{4,1,3,0,2:T(2,128)(2,1)S(1...) fusion(bf16[31,8,31,2,256]{4,1,3,0,2:T(8,128)(2,1)} %convert_bi, ...), kind=kLoop, calls=%fused_computation.63 | loop fusion | bytes 15745024 | tf_op jit(solution)/shard_map/split | solution.py:89
  1071.0 1.8 bitcast_dynamic-update-slice_fusion.8
  1072.8 1.8 bitcast_dynamic-update-slice_fusion.7
  1076.3 8.5 copy.181
  1084.8 5.5 all-to-all-start.1
  1090.4 23.4 %bitcast_convert_fusion = bf16[31,256,1024]{2,1,0:T(8,128)(2,1)} fusion(bf16[31,8,31,2,1024]{4,1,3,0,2:T(8,128)(2,1)} %all-gather.2.cloned.1.call-done, bf16[31,8,31,2,256]{4,3,2,0,1:T(2,128)(2,1)} %all-to-all-done.2), kind=kOutput, calls=%fused_computation.13 | convolution fusion | flops 8069578752 | bytes 55615488 | tf_op jit(solution)/shard_map/sntrc,sntrd->tcd/dot_general | solution.py:81
  1113.8 149.1 %all-to-all-done.1 = bf16[8,31,1,31,2,256]{5,4,3,2,1,0:T(2,128)(2,1)} async-done(((bf16[8,31,1,31,2,256]{5,4,3,2,1,0:T(2,128)(2,1)}), bf16[8,31,1,31,2,256]{5,4,3,2,1,0:T(2,128)(2,1)}, u32[]{:S(2)}, u32[]{:S(2)}) %all-to-all-start.1) | async-done | bytes 7872544 | tf_op jit(solution)/shard_map/all_to_all | solution.py:88
  1262.9 7.8 copy.182
  1270.7 17.9 %reshape_reshape.3 = bf16[31,248,512]{2,1,0:T(8,128)(2,1)} reshape(bf16[31,8,1,31,2,256]{5,4,3,1,0,2:T(2,128)(2,1)} %copy.182) | data formatting | bytes 15745024 | tf_op jit(solution)/shard_map/reshape;reshape | solution.py:96
  1288.6 13.9 %multiply_convert_fusion = bf16[31,240,512]{2,1,0:T(8,128)(2,1)} fusion(bf16[31,248,512]{2,1,0:T(8,128)(2,1)} %reshape_reshape.3, f32[240]{0:T(256)S(1)} %copy-done, bf16[31,248,240]{2,0,1:T(8,128)(2,1)} %bitcast_multiply_fusion.3), kind=kOutput, calls=%fused_computation.20 | convolution fusion | flops 1897021440 | bytes 19182272 | tf_op jit(solution)/shard_map/skj,skf->sjf/dot_general | solution.py:98
  1302.5 16.2 %reshape.248 = bf16[31,240,1,2,256]{4,3,1,0,2:T(2,128)(2,1)} reshape(bf16[31,240,512]{2,1,0:T(8,128)(2,1)} %multiply_convert_fusion) | data formatting | bytes 15237120 | tf_op jit(solution)/shard_map/reshape | solution.py:102
  (1223 shorter events, 329.0 us)
Async XLA Ops:
  7.2 1016.7 %all-gather.2.cloned.1.call-start = ((), (), s32[]{:S(2)}) async-start(), calls=%async_computation.3 | async-start | bytes 39362560 | tf_op jit(solution)/shard_map/all_gather | solution.py:80
  839.2 245.6 %all-to-all-start.2 = ((bf16[31,8,31,2,256]{4,3,2,0,1:T(2,128)(2,1)}), bf16[31,8,31,2,256]{4,3,2,0,1:T(2,128)(2,1)}, u32[]{:S(2)}, u32[]{:S(2)}) async-start(bf16[31,8,31,2,256]{4,3,2,0,1:T(2,128)(2,1)} %copy.185), calls=%async_computation.2 | async-start | bytes 15745024 | tf_op jit(solution)/shard_map/all_to_all | solution.py:77
  1084.8 178.0 %all-to-all-start.1 = ((bf16[8,31,1,31,2,256]{5,4,3,2,1,0:T(2,128)(2,1)}), bf16[8,31,1,31,2,256]{5,4,3,2,1,0:T(2,128)(2,1)}, u32[]{:S(2)}, u32[]{:S(2)}) async-start(bf16[8,31,1,31,2,256]{5,4,3,2,1,0:T(2,128)(2,1)} %copy.181), calls=%async_computation.1 | async-start | bytes 15745024 | tf_op jit(solution)/shard_map/all_to_all | solution.py:88
  1270.7 17.9 %copy-start = (f32[240]{0:T(256)S(1)}, f32[240]{0:T(256)}, u32[]{:S(2)}) copy-start(f32[240]{0:T(256)} %fusion.17) | copy-start | bytes 2884
Sparse Core Ops, SparseCore 0:
  831.6 192.1 all-gather.1
